TPU v7x, 32 devices: a whole 2x2x4 slice. The times are simulated.
32 devices in a mesh: step: 8 (over y, x, core), rows: 4 (over z).
Axes of the slice: x: 2, y: 2, z: 4, core: 2. Of those that a mesh axis runs over, the one named last changes fastest.
Arguments:
- init_states: float32 [8, 1, 2, 77, 384], P('step', None, None, None, 'rows'), may hold values from -63 to 63
- forcing: float32 [8, 1, 4, 384], P('step', None, None, 'rows'), may hold values from -63 to 63
- history: int32 [8, 1], P('step'), may hold values from 1 to 2
- land_mask: int32 [384], P('rows'), may hold values 0 or 1
- w_in: float32 [800, 158], replicated, may hold values from -0.5 to 0.5
- b_in: float32 [800], replicated, may hold values from -1.5 to 1.5
- w_dw: float32 [800, 7, 7], replicated, may hold values from -0.875 to 0.875
- bn_gain: float32 [800], replicated, may hold values from 0.5 to 1.5
- bn_bias: float32 [800], replicated, may hold values from -1.5 to 1.5
- w_up: float32 [3200, 800], replicated, may hold values from -0.21875 to 0.21875
- b_up: float32 [3200], replicated, may hold values from -1.5 to 1.5
- w_down: float32 [800, 3200], replicated, may hold values from -0.109375 to 0.109375
- b_down: float32 [800], replicated, may hold values from -1.5 to 1.5
- w_out: float32 [77, 800], replicated, may hold values from -0.21875 to 0.21875
- b_out: float32 [77], replicated, may hold values from -1.5 to 1.5
- cotangent: float32 [8, 8, 1, 77, 384], P('step', None, None, None, 'rows'), may hold values from -6 to 6
Outputs:
- predicted: float32 [8, 8, 1, 77, 384], P('step', None, None, None, 'rows')
- grad_init: float32 [8, 1, 2, 77, 384], P('step', None, None, None, 'rows')
- grad_forcing: float32 [8, 1, 4, 384], P('step', None, None, 'rows')
- grad_w_in: float32 [800, 158], replicated
- grad_b_in: float32 [800], replicated
- grad_w_dw: float32 [800, 7, 7], replicated
- grad_bn_gain: float32 [800], replicated
- grad_bn_bias: float32 [800], replicated
- grad_w_up: float32 [3200, 800], P('step', 'rows')
- grad_b_up: float32 [3200], replicated
- grad_w_down: float32 [800, 3200], P('rows', 'step')
- grad_b_down: float32 [800], replicated
- grad_w_out: float32 [77, 800], replicated
- grad_b_out: float32 [77], replicated
All inputs are finite; a program needn't handle non-finite values. No bound on the sum of `land_mask` on one device may be relied on, other than what follows from the above.
Results may differ from a plain program's by a relative error of at most 0.0003.
Values sent between devices are 32-bit elements; how exact they have to be, the bound alone decides.
No kernel may reach another device: no remote copies, remote signals or barrier semaphores. Data moves between devices by JAX's collectives and lax.ppermute only.
A program may use at most 448 MiB of HBM per device.

v0:
```python
import jax
import jax.numpy as jnp
from jax import lax
from jax.sharding import PartitionSpec as P

HALO = 3
ROLL = 8
COLS = 32
EPSILON = 1e-05
HIGHEST = lax.Precision.HIGHEST


def padded(cells, sides, width):
    for axis, dim in sides:
        count = lax.axis_size(axis)
        ends = count - 1
        head = lax.slice_in_dim(cells, 0, width, axis=dim)
        tail = lax.slice_in_dim(cells, cells.shape[dim] - width, cells.shape[dim], axis=dim)
        cells = jnp.concatenate(
            [
                lax.ppermute(tail, axis, [(i, (i + 1) % count) for i in range(ends)]),
                cells,
                lax.ppermute(head, axis, [((i + 1) % count, i) for i in range(ends)]),
            ],
            axis=dim,
        )
    return cells


def passed_along(x, axis, by):
    devices = lax.axis_size(axis)
    return lax.ppermute(x, axis, [(i, (i + by) % devices) for i in range(devices)])


def gelu_exact(values):
    return jax.nn.gelu(values, approximate=False)


def depthwise(extended, kernel):
    kernel_width = kernel.shape[-1]
    reach_rows = kernel_width // 2
    rows_out = extended.shape[-1] // COLS - 2 * reach_rows
    column = jnp.arange(extended.shape[-1]) % COLS
    accumulated = jnp.zeros(extended.shape[:-1] + (rows_out * COLS,), jnp.float32)
    for tap_col in range(kernel_width):
        offset = tap_col - reach_rows
        shifted = jnp.roll(extended, -offset, axis=-1)
        inside = (column + offset >= 0) & (column + offset < COLS)
        shifted = jnp.where(inside, shifted, jnp.zeros_like(shifted))
        for tap_row in range(kernel_width):
            piece = shifted[..., tap_row * COLS : (tap_row + rows_out) * COLS]
            accumulated = accumulated + kernel[:, tap_row, tap_col, None] * piece
    return accumulated


def contract(weights, values):
    return jnp.einsum("dc,bcp->bdp", weights, values, precision=HIGHEST)


def transposed(weights, values):
    return jnp.einsum("dc,bdp->bcp", weights, values, precision=HIGHEST)


def outer_sum(first_factor, second_factor):
    return jnp.einsum("bdp,bcp->dc", first_factor, second_factor, precision=HIGHEST)


def reduce_forces(grad_forces):
    accumulated = grad_forces[0]
    for grad_force in grad_forces[1:]:
        accumulated = accumulated + grad_force
    return accumulated


def per_device(
    init_states,
    forcing,
    history,
    land_mask,
    w_in,
    b_in,
    w_dw,
    bn_gain,
    bn_bias,
    w_up,
    b_up,
    w_down,
    b_down,
    w_out,
    b_out,
    cotangent,
):
    ocean_mask = land_mask.astype(jnp.float32)
    local_count = jnp.sum(ocean_mask)
    states = w_out.shape[0]
    rim_cells = HALO * COLS

    def backward_tick(grad_new, kept_tick, grad_list):
        inputs_all, lifted_ext, normalized, inverse_std, ocean_count, residual = kept_tick
        (
            grad_w_in,
            grad_b_in,
            grad_w_dw,
            grad_bn_gain,
            grad_bn_bias,
            grad_w_up,
            grad_b_up,
            grad_w_down,
            grad_b_down,
            grad_w_out,
            grad_b_out,
        ) = grad_list
        grad_masked = grad_new * ocean_mask
        grad_b_out = grad_b_out + jnp.sum(grad_masked, axis=(0, 2))
        grad_w_out = grad_w_out + outer_sum(grad_masked, residual)
        grad_branch = transposed(w_out, grad_masked) * ocean_mask
        normed = normalized * bn_gain[:, None] + bn_bias[:, None]
        hidden_pre = contract(w_up, normed) + b_up[:, None]
        activated, gelu_back = jax.vjp(gelu_exact, hidden_pre)
        grad_b_down = grad_b_down + jnp.sum(grad_branch, axis=(0, 2))
        grad_w_down = grad_w_down + outer_sum(grad_branch, activated)
        grad_hidden = gelu_back(transposed(w_down, grad_branch))[0]
        grad_b_up = grad_b_up + jnp.sum(grad_hidden, axis=(0, 2))
        grad_w_up = grad_w_up + outer_sum(grad_hidden, normed)
        grad_normed = transposed(w_up, grad_hidden)
        local_bias = jnp.sum(grad_normed, axis=-1)
        local_gain = jnp.sum(grad_normed * normalized, axis=-1)
        grad_bn_bias = grad_bn_bias + jnp.sum(local_bias, axis=0)
        grad_bn_gain = grad_bn_gain + jnp.sum(local_gain, axis=0)
        total_bias, total_gain = lax.psum((local_bias, local_gain), "rows")
        correction = (
            ocean_mask * (total_bias[..., None] + normalized * total_gain[..., None]) / ocean_count
        )
        grad_mixed = inverse_std[..., None] * bn_gain[:, None] * (grad_normed - correction)
        grad_ext = padded(grad_mixed, (("rows", 2),), rim_cells)
        grad_lifted = depthwise(grad_ext, w_dw[:, ::-1, ::-1]) + grad_branch
        unused_out, kernel_back = jax.vjp(lambda kernel: depthwise(lifted_ext, kernel), w_dw)
        grad_w_dw = grad_w_dw + kernel_back(grad_mixed)[0]
        grad_b_in = grad_b_in + jnp.sum(grad_lifted, axis=(0, 2))
        grad_w_in = grad_w_in + outer_sum(grad_lifted, inputs_all)
        grad_inputs = transposed(w_in, grad_lifted)
        grad_list = (
            grad_w_in,
            grad_b_in,
            grad_w_dw,
            grad_bn_gain,
            grad_bn_bias,
            grad_w_up,
            grad_b_up,
            grad_w_down,
            grad_b_down,
            grad_w_out,
            grad_b_out,
        )
        return (
            grad_inputs[:, :states],
            grad_inputs[:, states : 2 * states],
            grad_inputs[:, 2 * states :],
            grad_list,
        )

    forcings = [forcing[0] for rollout_step in range(ROLL)]
    cotangents = [cotangent[0, rollout_step] for rollout_step in range(ROLL)]
    current = init_states[0, :, 1]
    previous = jnp.where(
        (history[0] == 2)[:, None, None], init_states[0, :, 0], init_states[0, :, 1]
    )
    outputs = []
    kept_all = []
    for rollout_step in range(ROLL):
        if rollout_step > 0:
            current, previous = passed_along((outputs[-1], current), "step", 1)
        inputs_all = jnp.concatenate([previous, current, forcings[rollout_step]], axis=1)
        lifted = contract(w_in, inputs_all) + b_in[:, None]
        forward_lifted_ext = padded(lifted, (("rows", 2),), rim_cells)
        mixed_cells = depthwise(forward_lifted_ext, w_dw)
        first_sum = jnp.sum(mixed_cells * ocean_mask, axis=-1)
        second_sum = jnp.sum(mixed_cells * mixed_cells * ocean_mask, axis=-1)
        first_total, second_total, forward_ocean_count = lax.psum(
            (first_sum, second_sum, local_count), "rows"
        )
        forward_ocean_count = jnp.maximum(forward_ocean_count, 1.0)
        average = first_total / forward_ocean_count
        variance = second_total / forward_ocean_count - average * average
        forward_inverse_std = lax.rsqrt(variance + EPSILON)
        forward_normalized = (mixed_cells - average[..., None]) * forward_inverse_std[..., None]
        forward_normed = forward_normalized * bn_gain[:, None] + bn_bias[:, None]
        forward_hidden_pre = contract(w_up, forward_normed) + b_up[:, None]
        branch = contract(w_down, gelu_exact(forward_hidden_pre)) + b_down[:, None]
        forward_residual = (lifted + branch) * ocean_mask
        new_state = (contract(w_out, forward_residual) + b_out[:, None]) * ocean_mask
        new_state, kept_tick = (
            new_state,
            (
                inputs_all,
                forward_lifted_ext,
                forward_normalized,
                forward_inverse_std,
                forward_ocean_count,
                forward_residual,
            ),
        )
        outputs.append(new_state)
        kept_all.append(kept_tick)
    grad_list = (
        jnp.zeros_like(w_in),
        jnp.zeros_like(b_in),
        jnp.zeros_like(w_dw),
        jnp.zeros_like(bn_gain),
        jnp.zeros_like(bn_bias),
        jnp.zeros_like(w_up),
        jnp.zeros_like(b_up),
        jnp.zeros_like(w_down),
        jnp.zeros_like(b_down),
        jnp.zeros_like(w_out),
        jnp.zeros_like(b_out),
    )
    grad_forces = [None] * ROLL
    sent_cur = None
    sent_prev = None
    for rollout_step in reversed(range(ROLL)):
        grad_new = cotangents[rollout_step]
        if rollout_step < ROLL - 1:
            came_cur, came_prev = passed_along((sent_cur, sent_prev), "step", -1)
            grad_new = grad_new + came_cur
        grad_prev, grad_cur, grad_force, grad_list = backward_tick(
            grad_new, kept_all[rollout_step], grad_list
        )
        if rollout_step < ROLL - 1:
            grad_cur = grad_cur + came_prev
        sent_cur, sent_prev = (grad_cur, grad_prev)
        grad_forces[rollout_step] = grad_force
    single_history = (history[0] == 1)[:, None, None]
    double_history = (history[0] == 2)[:, None, None]
    grad_init_cur = sent_cur + jnp.where(single_history, sent_prev, jnp.zeros_like(sent_prev))
    grad_init_prev = jnp.where(double_history, sent_prev, jnp.zeros_like(sent_prev))
    grad_init = jnp.stack([grad_init_prev, grad_init_cur], axis=1)[None]
    predicted = jnp.stack(outputs, axis=0)[None]
    grad_forcing = reduce_forces(grad_forces)[None]
    (
        grad_w_in,
        grad_b_in,
        grad_w_dw,
        grad_bn_gain,
        grad_bn_bias,
        grad_w_up,
        grad_b_up,
        grad_w_down,
        grad_b_down,
        grad_w_out,
        grad_b_out,
    ) = grad_list
    small_totals = lax.psum(
        (
            grad_w_in,
            grad_b_in,
            grad_w_dw,
            grad_bn_gain,
            grad_bn_bias,
            grad_b_up,
            grad_b_down,
            grad_w_out,
            grad_b_out,
        ),
        ("step", "rows"),
    )
    shares = (
        lax.psum_scatter(grad_w_up, "step", scatter_dimension=0, tiled=True),
        lax.psum_scatter(grad_w_down, "step", scatter_dimension=1, tiled=True),
    )
    share_up, share_down = (
        lax.psum_scatter(shares[0], "rows", scatter_dimension=1, tiled=True),
        lax.psum_scatter(shares[1], "rows", scatter_dimension=0, tiled=True),
    )
    return (
        predicted,
        grad_init,
        grad_forcing,
        small_totals[0],
        small_totals[1],
        small_totals[2],
        small_totals[3],
        small_totals[4],
        share_up,
        small_totals[5],
        share_down,
        small_totals[6],
        small_totals[7],
        small_totals[8],
    )


def solution(mesh):
    in_specs = (
        P("step", None, None, None, "rows"),
        P("step", None, None, "rows"),
        P("step", None),
        P("rows"),
        P(),
        P(),
        P(),
        P(),
        P(),
        P(),
        P(),
        P(),
        P(),
        P(),
        P(),
        P("step", None, None, None, "rows"),
    )
    out_specs = (
        P("step", None, None, None, "rows"),
        P("step", None, None, None, "rows"),
        P("step", None, None, "rows"),
        P(),
        P(),
        P(),
        P(),
        P(),
        P("step", "rows"),
        P(),
        P("rows", "step"),
        P(),
        P(),
        P(),
    )
    return jax.shard_map(
        per_device, mesh=mesh, in_specs=in_specs, out_specs=out_specs, check_vma=False
    )
```

profile of v0, /device:TPU:0, one launch (start us, length us, event | category | flops | bytes accessed | tf_op | source)
XLA Modules:
  0.0 1748.8 jit_solution(15639221785140882595)
XLA Ops:
  58.7 16.4 fusion.392
  123.4 16.4 fusion.377
  188.8 16.4 fusion.362
  253.5 16.4 fusion.347
  317.9 16.4 fusion.332
  382.8 16.4 fusion.317
  448.6 16.4 fusion.302
  516.0 12.9 fusion.1177
  589.5 11.1 fusion.848
  757.7 13.4 fusion.43
  808.4 12.9 fusion.39
  833.9 13.5 fusion.35
  869.6 11.2 all-reduce.396
  885.3 12.9 fusion.31
  910.2 13.5 fusion.27
  945.8 11.5 all-reduce.395
  961.8 13.6 fusion.23
  988.9 15.0 fusion.19
  1016.1 28.3 %add_add_fusion.1 = f32[3200,800]{1,0:T(8,128)} fusion(f32[3200,800]{1,0:T(8,128)} %fusion.19, f32[3200,800]{1,0:T(8,128)} %fusion.23, f32[3200,800]{1,0:T(8,128)} %fusion.27, f32[3200,800]{1,0:T(8,128)} %fusion.31, f32[3200,800]{1,0:T(8,128)} %fusion.35, f32[3200,800]{1,0:T(8,128)S(1)} %bitcast.1892, f32[3200,800]{1,0:T(8,128)} %fusion.39, ...), kind=kOutput, calls=%fused_computation.1 | convolution fusion | flops 2967347200 | bytes 83468800 | tf_op jit(solution)/shard_map/bdp,bcp->dc/dot_general | solution.py:65
  1045.4 13.5 fusion.47
  1058.9 17.4 fusion.57
  1076.4 17.5 fusion.67
  1093.8 17.9 %fusion.77 = f32[800,3200]{0,1:T(8,128)} fusion(f32[1,96,3200]{2,1,0:T(8,128)S(1)} %copy-done.225, f32[1,96,800]{2,1,0:T(8,128)S(1)} %copy-done.186), kind=kOutput, calls=%fused_computation.128 | convolution fusion | flops 2968780800 | bytes 11776000 | tf_op jit(solution)/shard_map/bdp,bcp->dc/dot_general | solution.py:65
  1111.8 17.4 fusion.87
  1129.2 17.4 fusion.97
  1146.6 17.6 %fusion.107 = f32[800,3200]{0,1:T(8,128)} fusion(f32[1,96,3200]{2,1,0:T(8,128)S(1)} %copy-done.216, f32[1,96,800]{2,1,0:T(8,128)S(1)} %copy-done.193), kind=kOutput, calls=%fused_computation.176 | convolution fusion | flops 2968780800 | bytes 11776000 | tf_op jit(solution)/shard_map/bdp,bcp->dc/dot_general | solution.py:65
  1164.2 29.4 %add_add_fusion = f32[800,3200]{0,1:T(8,128)} fusion(f32[800,3200]{0,1:T(8,128)} %fusion.107, f32[800,3200]{0,1:T(8,128)} %fusion.97, f32[800,3200]{0,1:T(8,128)} %fusion.87, f32[800,3200]{0,1:T(8,128)} %fusion.77, f32[800,3200]{0,1:T(8,128)} %fusion.67, f32[800,3200]{0,1:T(8,128)S(1)} %fusion.47, f32[800,3200]{0,1:T(8,128)} %fusion.57, ...), kind=kOutput, calls=%fused_computation | convolution fusion | flops 2986700800 | bytes 83456000 | tf_op jit(solution)/shard_map/bdp,bcp->dc/dot_general | solution.py:65
  1227.0 16.6 fusion.287
  1434.4 11.5 all-reduce.394
  1454.5 105.7 %add_add_fusion.2 = f32[800,7,7]{0,2,1:T(8,128)} fusion(f32[800,1,1]{0,2,1:T(1,128)S(1)} %broadcast_in_dim.2494, f32[800,1,1]{0,2,1:T(1,128)S(1)} %broadcast_in_dim.2493, f32[800,1,1]{0,2,1:T(1,128)S(1)} %broadcast_in_dim.2492, f32[800,1,1]{0,2,1:T(1,128)S(1)} %broadcast_in_dim.2491, f32[800,1,1]{0,2,1:T(1,128)S(1)} %broadcast_in_dim.2490, ...), kind=kLoop, calls=%fused_computation.1873 | loop fusion | flops 13720000 | bytes 1587200 | tf_op jit(solution)/shard_map/add | solution.py:138
  1591.5 42.2 %all-reduce.392 = (f32[800]{0:T(1024)}, f32[800]{0:T(1024)}, f32[800]{0:T(1024)}, f32[3200]{0:T(1024)}, f32[800]{0:T(1024)}, /*index=5*/f32[77]{0:T(128)}) all-reduce(f32[800]{0:T(1024)S(1)} %add_add_fusion.8, f32[800]{0:T(1024)S(1)} %add_add_fusion.7, ...), channel_id=1, replica_groups=mesh['step'=8,'rows'=4] {'step','rows'}, use_global_device_ids=true, to_apply=%region_75.76 | all-reduce | flops 6477 | bytes 51816 | tf_op jit(solution)/shard_map/psum | solution.py:253
  1637.0 101.1 %all-reduce.412.cloned.1.call-done = (f32[800,158]{0,1:T(8,128)}, f32[800,7,7]{0,2,1:T(8,128)}, f32[77,800]{1,0:T(8,128)}) async-done(((f32[800,158]{0,1:T(8,128)}, f32[800,7,7]{0,2,1:T(8,128)}, f32[77,800]{1,0:T(8,128)}), (f32[800,158]{0,1:T(8,128)}, f32[800,7,7]{0,2,1:T(8,128)}, f32[77,800]{1,0:T(8,128)})) %all-reduce.412.cloned.1.call-update) | async-done | bytes 908816 | tf_op jit(solution)/shard_map/psum | solution.py:253
  (2054 shorter events, 1012.4 us)
Async XLA Ops:
  8.0 1558.9 %reduce-scatter.9.cloned.1.call-start = ((), (), s32[]{:S(2)}) async-start(), calls=%async_computation.4 | async-start | bytes 12902400 | tf_op jit(solution)/shard_map/reduce_scatter | solution.py:268
  9.2 67.4 %collective-permute-start.2 = (f32[1,77,96]{2,1,0:T(8,128)S(1)}, f32[1,77,96]{2,1,0:T(8,128)S(1)}, u32[]{:S(2)}, u32[]{:S(2)}) collective-permute-start(f32[1,77,96]{2,1,0:T(8,128)S(1)} %bitcast.1912), channel_id=1, source_target_pairs={{0,4},{4,8},{8,12},{12,16},{16,20},{20,24},{24,28},{28,0},{1,5},{5... | collective-permute-start | bytes 88712 | tf_op jit(solution)/shard_map/ppermute | solution.py:32
  11.6 13.0 collective-permute-start.1
  16.1 12.6 collective-permute-start
  85.3 55.9 %collective-permute-start.6 = (f32[1,77,96]{2,1,0:T(8,128)S(1)}, f32[1,77,96]{2,1,0:T(8,128)S(1)}, u32[]{:S(2)}, u32[]{:S(2)}) collective-permute-start(f32[1,77,96]{2,1,0:T(8,128)S(1)} %collective-permute-done.3), channel_id=1, source_target_pairs={{0,4},{4,8},{8,12},{12,16},{16,20},{20,24},{24,28},{28,0},{1,5},{5... | collective-permute-start | bytes 88712 | tf_op jit(solution)/shard_map/ppermute | solution.py:32
  150.9 55.9 %collective-permute-start.10 = (f32[1,77,96]{2,1,0:T(8,128)S(1)}, f32[1,77,96]{2,1,0:T(8,128)S(1)}, u32[]{:S(2)}, u32[]{:S(2)}) collective-permute-start(f32[1,77,96]{2,1,0:T(8,128)S(1)} %collective-permute-done.7), channel_id=1, source_target_pairs={{0,4},{4,8},{8,12},{12,16},{16,20},{20,24},{24,28},{28,0},{1,5},{5... | collective-permute-start | bytes 88712 | tf_op jit(solution)/shard_map/ppermute | solution.py:32
  216.6 54.8 %collective-permute-start.14 = (f32[1,77,96]{2,1,0:T(8,128)S(1)}, f32[1,77,96]{2,1,0:T(8,128)S(1)}, u32[]{:S(2)}, u32[]{:S(2)}) collective-permute-start(f32[1,77,96]{2,1,0:T(8,128)S(1)} %collective-permute-done.11), channel_id=1, source_target_pairs={{0,4},{4,8},{8,12},{12,16},{16,20},{20,24},{24,28},{28,0},{1,5},{5... | collective-permute-start | bytes 88712 | tf_op jit(solution)/shard_map/ppermute | solution.py:32
  281.0 54.7 %collective-permute-start.18 = (f32[1,77,96]{2,1,0:T(8,128)S(1)}, f32[1,77,96]{2,1,0:T(8,128)S(1)}, u32[]{:S(2)}, u32[]{:S(2)}) collective-permute-start(f32[1,77,96]{2,1,0:T(8,128)S(1)} %collective-permute-done.15), channel_id=1, source_target_pairs={{0,4},{4,8},{8,12},{12,16},{16,20},{20,24},{24,28},{28,0},{1,5},{5... | collective-permute-start | bytes 88712 | tf_op jit(solution)/shard_map/ppermute | solution.py:32
  345.5 55.4 %collective-permute-start.22 = (f32[1,77,96]{2,1,0:T(8,128)S(1)}, f32[1,77,96]{2,1,0:T(8,128)S(1)}, u32[]{:S(2)}, u32[]{:S(2)}) collective-permute-start(f32[1,77,96]{2,1,0:T(8,128)S(1)} %collective-permute-done.19), channel_id=1, source_target_pairs={{0,4},{4,8},{8,12},{12,16},{16,20},{20,24},{24,28},{28,0},{1,5},{5... | collective-permute-start | bytes 88712 | tf_op jit(solution)/shard_map/ppermute | solution.py:32
  410.6 56.7 %collective-permute-start.26 = (f32[1,77,96]{2,1,0:T(8,128)S(1)}, f32[1,77,96]{2,1,0:T(8,128)S(1)}, u32[]{:S(2)}, u32[]{:S(2)}) collective-permute-start(f32[1,77,96]{2,1,0:T(8,128)S(1)} %collective-permute-done.23), channel_id=1, source_target_pairs={{0,4},{4,8},{8,12},{12,16},{16,20},{20,24},{24,28},{28,0},{1,5},{5... | collective-permute-start | bytes 88712 | tf_op jit(solution)/shard_map/ppermute | solution.py:32
  617.5 20.8 %collective-permute-start.35 = (f32[1,77,96]{2,1,0:T(8,128)S(1)}, f32[1,77,96]{2,1,0:T(8,128)S(1)}, u32[]{:S(2)}, u32[]{:S(2)}) collective-permute-start(f32[1,77,96]{2,1,0:T(8,128)S(1)} %get-tuple-element.916), channel_id=1, source_target_pairs={{0,28},{4,0},{8,4},{12,8},{16,12},{20,16},{24,20},{28,24},{1,29},{... | collective-permute-start | bytes 88712 | tf_op jit(solution)/shard_map/ppermute | solution.py:32
  676.9 21.0 %collective-permute-start.39 = (f32[1,77,96]{2,1,0:T(8,128)S(1)}, f32[1,77,96]{2,1,0:T(8,128)S(1)}, u32[]{:S(2)}, u32[]{:S(2)}) collective-permute-start(f32[1,77,96]{2,1,0:T(8,128)S(1)} %get-tuple-element.913), channel_id=1, source_target_pairs={{0,28},{4,0},{8,4},{12,8},{16,12},{20,16},{24,20},{28,24},{1,29},{... | collective-permute-start | bytes 88712 | tf_op jit(solution)/shard_map/ppermute | solution.py:32
  735.4 11.2 collective-permute-start.41
  736.7 20.5 %collective-permute-start.43 = (f32[1,77,96]{2,1,0:T(8,128)S(1)}, f32[1,77,96]{2,1,0:T(8,128)S(1)}, u32[]{:S(2)}, u32[]{:S(2)}) collective-permute-start(f32[1,77,96]{2,1,0:T(8,128)S(1)} %get-tuple-element.912), channel_id=1, source_target_pairs={{0,28},{4,0},{8,4},{12,8},{16,12},{20,16},{24,20},{28,24},{1,29},{... | collective-permute-start | bytes 88712 | tf_op jit(solution)/shard_map/ppermute | solution.py:32
  757.4 13.8 collective-permute-start.44
  803.5 18.0 %collective-permute-start.46 = (f32[1,800,96]{1,2,0:T(8,128)S(1)}, f32[1,800,96]{1,2,0:T(8,128)S(1)}, u32[]{:S(2)}, u32[]{:S(2)}) collective-permute-start(f32[1,800,96]{1,2,0:T(8,128)S(1)} %get-tuple-element.753), channel_id=1, source_target_pairs={{0,1},{1,2},{2,3},{4,5},{5,6},{6,7},{8,9},{9,10},{10,11},{12,13},{... | collective-permute-start | bytes 921608 | tf_op jit(solution)/shard_map/ppermute | solution.py:21
  807.1 14.5 collective-permute-start.45
  832.3 15.1 collective-permute-start.48
  882.6 15.8 collective-permute-start.50
  884.0 14.5 collective-permute-start.49
  898.2 10.9 collective-permute-start.51
  909.2 14.5 collective-permute-start.52
  959.2 16.5 collective-permute-start.54
  960.5 15.2 collective-permute-start.53
  975.4 10.9 collective-permute-start.55
  987.0 17.0 collective-permute-start.56
  1044.4 536.2 %reduce-scatter.11.cloned.1.call-start = ((), (), s32[]{:S(2)}) async-start(), calls=%async_computation.5 | async-start | bytes 12902400 | tf_op jit(solution)/shard_map/reduce_scatter | solution.py:269
  1193.7 441.3 %reduce-scatter.13.cloned.1.call-start = ((), (), s32[]{:S(2)}) async-start(), calls=%async_computation.6 | async-start | bytes 2048000
  1447.1 116.1 %collective-permute-start.58 = (f32[1,800,96]{1,2,0:T(8,128)S(1)}, f32[1,800,96]{1,2,0:T(8,128)S(1)}, u32[]{:S(2)}, u32[]{:S(2)}) collective-permute-start(f32[1,800,96]{1,2,0:T(8,128)S(1)} %get-tuple-element.756), channel_id=1, source_target_pairs={{0,1},{1,2},{2,3},{4,5},{5,6},{6,7},{8,9},{9,10},{10,11},{12,13},{... | collective-permute-start | bytes 921608 | tf_op jit(solution)/shard_map/ppermute | solution.py:21
  1448.4 114.8 %collective-permute-start.57 = (f32[1,800,96]{1,2,0:T(8,128)S(1)}, f32[1,800,96]{1,2,0:T(8,128)S(1)}, u32[]{:S(2)}, u32[]{:S(2)}) collective-permute-start(f32[1,800,96]{1,2,0:T(8,128)S(1)} %get-tuple-element.756), channel_id=1, source_target_pairs={{1,0},{2,1},{3,2},{5,4},{6,5},{7,6},{9,8},{10,9},{11,10},{13,12},{... | collective-permute-start | bytes 921608 | tf_op jit(solution)/shard_map/ppermute | solution.py:23
  1570.0 168.0 %all-reduce.412.cloned.1.call-start = ((), (), s32[]{:S(2)}) async-start(), calls=%async_computation.8 | async-start | bytes 2121728 | tf_op jit(solution)/shard_map/psum | solution.py:253
  1580.6 157.5 %reduce-scatter.15.cloned.1.call-start = ((), (), s32[]{:S(2)}) async-start(), calls=%async_computation.7 | async-start | bytes 2048000
  (559 other events, 7228.0 us)
Sparse Core Ops, SparseCore 0:
  1044.6 85.5 reduce-scatter.8
  1193.9 85.3 reduce-scatter.10
  1570.2 37.0 reduce-scatter.12
  1610.0 36.3 reduce-scatter.14
Sparse Core Ops, SparseCore 1:
  1580.6 157.4 all-reduce.411
where the time goes:
time: 1760 us; the launch traced here: 1750 us
  matrix products  694 us (39%)
  other arithmetic  298 us (17%)
  waiting for transfers between devices  231 us (13%)
  local copies, waits for them, and re-layouts  224 us (13%)
  blocking collectives  194 us (11%)
  starting transfers between devices  81 us (5%)
  between operations  26.5 us (2%)
    dot_general x32, matrix products, outer_sum(): jnp.einsum('bdp,bcp->dc', first_factor, second_factor, precision=HIGHEST)  289 us
    dot_general x32, matrix products, contract(): return jnp.einsum('dc,bcp->bdp', weights, values, precision=HIGHEST)  224 us
    dot_general x32, matrix products, transposed(): return jnp.einsum('dc,bdp->bcp', weights, values, precision=HIGHEST)  181 us
    broadcast_in_dim x392, local copies, waits for them, and re-layouts, depthwise(): accumulated = accumulated + kernel[:, tap_row, tap_col, None] * piece  178 us
    add x1, other arithmetic, backward_tick(): grad_w_dw = grad_w_dw + kernel_back(grad_mixed)[0]  106 us
    psum x1, waiting for transfers between devices, per_device(): lax.psum((grad_w_in, grad_b_in, grad_w_dw, grad_bn_gain, grad_bn_bias, gr...  101 us
    select_n x109, other arithmetic, depthwise(): shifted = jnp.where(inside, shifted, jnp.zeros_like(shifted))  89.6 us
    psum x8, blocking collectives, backward_tick(): total_bias, total_gain = lax.psum((local_bias, local_gain), 'rows')  79.3 us
  transfers between devices with their start and end apart: 65, of which 34 were waited for; matrix products, arithmetic and copies ran while one was open for 54% of the time, Pallas kernels for 0%

commit v1 on v0

--- a/solution.py
+++ b/solution.py
@@ -251,18 +251,21 @@
         grad_b_out,
     ) = grad_list
     small_totals = lax.psum(
-        (
-            grad_w_in,
-            grad_b_in,
-            grad_w_dw,
-            grad_bn_gain,
-            grad_bn_bias,
-            grad_b_up,
-            grad_b_down,
-            grad_w_out,
-            grad_b_out,
+        lax.psum(
+            (
+                grad_w_in,
+                grad_b_in,
+                grad_w_dw,
+                grad_bn_gain,
+                grad_bn_bias,
+                grad_b_up,
+                grad_b_down,
+                grad_w_out,
+                grad_b_out,
+            ),
+            "rows",
         ),
-        ("step", "rows"),
+        "step",
     )
     shares = (
         lax.psum_scatter(grad_w_up, "step", scatter_dimension=0, tiled=True),

time: 1760 us -> 1820 us (1.034)
  waiting for transfers between devices: 231 us -> 263 us
  local copies, waits for them, and re-layouts: 224 us -> 247 us
    psum x1, waiting for transfers between devices: 101 us -> 16.7 us  [per_device(): lax.psum((grad_w_in, grad_b_in, grad_w_dw, grad_bn_gain, grad_bn_bias, gr...]
    reduce_scatter x1, waiting for transfers between devices: 0.02 us -> 65.3 us  [per_device(): lax.psum_scatter(grad_w_down, 'step', scatter_dimension=1, tiled=True)]
    psum x0 -> x1, waiting for transfers between devices: none -> 41.5 us  [per_device(): lax.psum(lax.psum((grad_w_in, grad_b_in, grad_w_dw, grad_bn_gain, grad_bn...]
    unnamed x7 -> x8, waiting for transfers between devices: 0.09 us -> 38.8 us
    psum x0 -> x1, blocking collectives: none -> 23.3 us  [per_device(): lax.psum(lax.psum((grad_w_in, grad_b_in, grad_w_dw, grad_bn_gain, grad_bn...]
    broadcast_in_dim x392, local copies, waits for them, and re-layouts: 178 us -> 200 us  [depthwise(): accumulated = accumulated + kernel[:, tap_row, tap_col, None] * piece]
    psum x1, blocking collectives: 42.2 us -> 21.7 us  [per_device(): lax.psum((grad_w_in, grad_b_in, grad_w_dw, grad_bn_gain, grad_bn_bias, gr...]
  transfers between devices with their start and end apart: 65 -> 66, of which waited for: 34 -> 31; matrix products, arithmetic and copies ran while one was open for 54% -> 53% of each run, Pallas kernels for 0% -> 0%
where the time goes in v1:
time: 1820 us; the launch traced here: 1810 us
  matrix products  693 us (38%)
  other arithmetic  291 us (16%)
  waiting for transfers between devices  263 us (14%)
  local copies, waits for them, and re-layouts  247 us (14%)
  blocking collectives  208 us (11%)
  starting transfers between devices  77.5 us (4%)
  between operations  26.5 us (1%)
    dot_general x32, matrix products, outer_sum(): jnp.einsum('bdp,bcp->dc', first_factor, second_factor, precision=HIGHEST)  296 us
    dot_general x32, matrix products, contract(): return jnp.einsum('dc,bcp->bdp', weights, values, precision=HIGHEST)  220 us
    broadcast_in_dim x392, local copies, waits for them, and re-layouts, depthwise(): accumulated = accumulated + kernel[:, tap_row, tap_col, None] * piece  200 us
    dot_general x32, matrix products, transposed(): return jnp.einsum('dc,bdp->bcp', weights, values, precision=HIGHEST)  177 us
    add x1, other arithmetic, backward_tick(): grad_w_dw = grad_w_dw + kernel_back(grad_mixed)[0]  105 us
    psum x8, blocking collectives, backward_tick(): total_bias, total_gain = lax.psum((local_bias, local_gain), 'rows')  89.5 us
    select_n x109, other arithmetic, depthwise(): shifted = jnp.where(inside, shifted, jnp.zeros_like(shifted))  89.4 us
    psum x8, blocking collectives, per_device(): lax.psum((first_sum, second_sum, local_count), 'rows')  73.6 us
  transfers between devices with their start and end apart: 66, of which 31 were waited for; matrix products, arithmetic and copies ran while one was open for 53% of the time, Pallas kernels for 0%

profile of v1, /device:TPU:0, one launch (start us, length us, event | category | flops | bytes accessed | tf_op | source)
XLA Modules:
  0.0 1805.5 jit_solution(15351352176004870192)
XLA Ops:
  58.0 16.4 fusion.392
  121.5 16.4 fusion.377
  185.5 16.4 fusion.362
  249.9 16.4 fusion.347
  313.1 16.4 fusion.332
  376.6 16.4 fusion.317
  444.0 16.4 fusion.302
  512.4 17.1 fusion.287
  567.9 12.9 fusion.43
  580.8 17.4 fusion.47
  682.9 12.9 fusion.39
  695.9 17.4 fusion.57
  932.8 12.9 fusion.35
  965.6 12.5 fusion.1173
  1007.3 13.2 fusion.31
  1032.2 14.9 fusion.27
  1085.5 13.7 fusion.23
  1112.0 15.0 fusion.19
  1138.4 28.2 %add_add_fusion.1 = f32[3200,800]{1,0:T(8,128)} fusion(f32[3200,800]{1,0:T(8,128)} %fusion.19, f32[3200,800]{1,0:T(8,128)} %fusion.23, f32[3200,800]{1,0:T(8,128)} %fusion.27, f32[3200,800]{1,0:T(8,128)} %fusion.31, f32[3200,800]{1,0:T(8,128)} %fusion.35, f32[3200,800]{1,0:T(8,128)S(1)} %bitcast.1892, f32[3200,800]{1,0:T(8,128)} %fusion.39, ...), kind=kOutput, calls=%fused_computation.1 | convolution fusion | flops 2967347200 | bytes 83468800 | tf_op jit(solution)/shard_map/bdp,bcp->dc/dot_general | solution.py:65
  1167.6 18.8 %fusion.67 = f32[800,3200]{0,1:T(8,128)} fusion(f32[1,96,3200]{2,1,0:T(8,128)} %copy-done.214, f32[1,96,800]{2,1,0:T(8,128)S(1)} %copy-done.165), kind=kOutput, calls=%fused_computation.112 | convolution fusion | flops 2968780800 | bytes 11776000 | tf_op jit(solution)/shard_map/bdp,bcp->dc/dot_general | solution.py:65
  1220.3 17.4 fusion.77
  1271.6 17.6 fusion.87
  1323.1 17.4 fusion.97
  1372.4 17.9 fusion.107
  1421.2 105.0 %add_add_fusion.2 = f32[800,7,7]{0,2,1:T(8,128)} fusion(f32[800,1,1]{0,2,1:T(1,128)S(1)} %broadcast_in_dim.2494, f32[800,1,1]{0,2,1:T(1,128)S(1)} %broadcast_in_dim.2493, f32[800,1,1]{0,2,1:T(1,128)S(1)} %broadcast_in_dim.2492, f32[800,1,1]{0,2,1:T(1,128)S(1)} %broadcast_in_dim.2491, f32[800,1,1]{0,2,1:T(1,128)S(1)} %broadcast_in_dim.2490, ...), kind=kLoop, calls=%fused_computation.1873 | loop fusion | flops 13720000 | bytes 1587200 | tf_op jit(solution)/shard_map/add | solution.py:138
  1538.1 32.4 %add_add_fusion = f32[800,3200]{0,1:T(8,128)} fusion(f32[800,3200]{0,1:T(8,128)} %fusion.107, f32[800,3200]{0,1:T(8,128)} %fusion.97, f32[800,3200]{0,1:T(8,128)} %fusion.87, f32[800,3200]{0,1:T(8,128)} %fusion.77, f32[800,3200]{0,1:T(8,128)} %fusion.67, f32[800,3200]{0,1:T(8,128)} %fusion.47, f32[800,3200]{0,1:T(8,128)} %fusion.57, ...), kind=kOutput, calls=%fused_computation | convolution fusion | flops 2986700800 | bytes 83456000 | tf_op jit(solution)/shard_map/bdp,bcp->dc/dot_general | solution.py:65
  1573.7 16.7 all-reduce.417.cloned.1.call-done
  1590.7 65.3 %reduce-scatter.11.cloned.1.call-done = f32[800,400]{0,1:T(8,128)} async-done(((f32[800,3200]{0,1:T(8,128)}), f32[800,400]{0,1:T(8,128)}) %reduce-scatter.11.cloned.1.call-update) | async-done | bytes 1280016 | tf_op jit(solution)/shard_map/reduce_scatter | solution.py:272
  1666.4 21.7 %all-reduce.394 = (f32[800]{0:T(1024)S(1)}, f32[800]{0:T(1024)S(1)}, f32[800]{0:T(1024)S(1)}, f32[3200]{0:T(1024)S(1)}, f32[800]{0:T(1024)S(1)}, /*index=5*/f32[77]{0:T(128)S(1)}) all-reduce(f32[800]{0:T(1024)S(1)} %add_add_fusion.8, f32[800]{0:T(1024)S(1)} %add_add_fusion.7, ...), channel_id=1, replica_groups=mesh['step'=8,'rows'=4] {'rows'}, use_global_device_ids=true, to_apply=%region_76.77 | all-reduce | flops 6477 | bytes 51816 | tf_op jit(solution)/shard_map/psum | solution.py:254
  1688.1 23.3 %all-reduce.392 = (f32[800]{0:T(1024)}, f32[800]{0:T(1024)}, f32[800]{0:T(1024)}, f32[3200]{0:T(1024)}, f32[800]{0:T(1024)}, /*index=5*/f32[77]{0:T(128)}) all-reduce(f32[800]{0:T(1024)S(1)} %get-tuple-element.700, f32[800]{0:T(1024)S(1)} %get-tuple-element.701, ...), channel_id=1, replica_groups=mesh['step'=8,'rows'=4] {'step'}, use_global_device_ids=true, to_apply=%region_77.78 | all-reduce | flops 6477 | bytes 51816 | tf_op jit(solution)/shard_map/psum | solution.py:253
  1714.6 41.5 %all-reduce.415.cloned.1.call-done = (f32[800,158]{0,1:T(8,128)}, f32[800,7,7]{0,2,1:T(8,128)}, f32[77,800]{1,0:T(8,128)}) async-done(((f32[800,158]{0,1:T(8,128)}, f32[800,7,7]{0,2,1:T(8,128)}, f32[77,800]{1,0:T(8,128)}), (f32[800,158]{0,1:T(8,128)}, f32[800,7,7]{0,2,1:T(8,128)}, f32[77,800]{1,0:T(8,128)})) %all-reduce.415.cloned.1.call-update) | async-done | bytes 908816 | tf_op jit(solution)/shard_map/psum | solution.py:253
  1756.2 38.7 %reduce-scatter.15.cloned.1.call-done = f32[200,400]{1,0:T(8,128)} async-done(((f32[800,400]{1,0:T(8,128)}), f32[200,400]{1,0:T(8,128)}) %reduce-scatter.15.cloned.1.call-update) | async-done | bytes 320016
  (2156 shorter events, 1042.4 us)
Async XLA Ops:
  8.0 1562.5 %reduce-scatter.9.cloned.1.call-start = ((), (), s32[]{:S(2)}) async-start(), calls=%async_computation.4 | async-start | bytes 12902400 | tf_op jit(solution)/shard_map/reduce_scatter | solution.py:271
  9.2 66.0 %collective-permute-start.2 = (f32[1,77,96]{2,1,0:T(8,128)S(1)}, f32[1,77,96]{2,1,0:T(8,128)S(1)}, u32[]{:S(2)}, u32[]{:S(2)}) collective-permute-start(f32[1,77,96]{2,1,0:T(8,128)S(1)} %bitcast.1912), channel_id=1, source_target_pairs={{0,4},{4,8},{8,12},{12,16},{16,20},{20,24},{24,28},{28,0},{1,5},{5... | collective-permute-start | bytes 88712 | tf_op jit(solution)/shard_map/ppermute | solution.py:32
  83.9 54.9 %collective-permute-start.6 = (f32[1,77,96]{2,1,0:T(8,128)S(1)}, f32[1,77,96]{2,1,0:T(8,128)S(1)}, u32[]{:S(2)}, u32[]{:S(2)}) collective-permute-start(f32[1,77,96]{2,1,0:T(8,128)S(1)} %collective-permute-done.3), channel_id=1, source_target_pairs={{0,4},{4,8},{8,12},{12,16},{16,20},{20,24},{24,28},{28,0},{1,5},{5... | collective-permute-start | bytes 88712 | tf_op jit(solution)/shard_map/ppermute | solution.py:32
  148.6 54.1 %collective-permute-start.10 = (f32[1,77,96]{2,1,0:T(8,128)S(1)}, f32[1,77,96]{2,1,0:T(8,128)S(1)}, u32[]{:S(2)}, u32[]{:S(2)}) collective-permute-start(f32[1,77,96]{2,1,0:T(8,128)S(1)} %collective-permute-done.7), channel_id=1, source_target_pairs={{0,4},{4,8},{8,12},{12,16},{16,20},{20,24},{24,28},{28,0},{1,5},{5... | collective-permute-start | bytes 88712 | tf_op jit(solution)/shard_map/ppermute | solution.py:32
  212.4 54.6 %collective-permute-start.14 = (f32[1,77,96]{2,1,0:T(8,128)S(1)}, f32[1,77,96]{2,1,0:T(8,128)S(1)}, u32[]{:S(2)}, u32[]{:S(2)}) collective-permute-start(f32[1,77,96]{2,1,0:T(8,128)S(1)} %collective-permute-done.11), channel_id=1, source_target_pairs={{0,4},{4,8},{8,12},{12,16},{16,20},{20,24},{24,28},{28,0},{1,5},{5... | collective-permute-start | bytes 88712 | tf_op jit(solution)/shard_map/ppermute | solution.py:32
  276.7 53.7 %collective-permute-start.18 = (f32[1,77,96]{2,1,0:T(8,128)S(1)}, f32[1,77,96]{2,1,0:T(8,128)S(1)}, u32[]{:S(2)}, u32[]{:S(2)}) collective-permute-start(f32[1,77,96]{2,1,0:T(8,128)S(1)} %collective-permute-done.15), channel_id=1, source_target_pairs={{0,4},{4,8},{8,12},{12,16},{16,20},{20,24},{24,28},{28,0},{1,5},{5... | collective-permute-start | bytes 88712 | tf_op jit(solution)/shard_map/ppermute | solution.py:32
  340.2 53.6 %collective-permute-start.22 = (f32[1,77,96]{2,1,0:T(8,128)S(1)}, f32[1,77,96]{2,1,0:T(8,128)S(1)}, u32[]{:S(2)}, u32[]{:S(2)}) collective-permute-start(f32[1,77,96]{2,1,0:T(8,128)S(1)} %collective-permute-done.19), channel_id=1, source_target_pairs={{0,4},{4,8},{8,12},{12,16},{16,20},{20,24},{24,28},{28,0},{1,5},{5... | collective-permute-start | bytes 88712 | tf_op jit(solution)/shard_map/ppermute | solution.py:32
  404.4 57.3 %collective-permute-start.26 = (f32[1,77,96]{2,1,0:T(8,128)}, f32[1,77,96]{2,1,0:T(8,128)S(1)}, u32[]{:S(2)}, u32[]{:S(2)}) collective-permute-start(f32[1,77,96]{2,1,0:T(8,128)} %collective-permute-done.23), channel_id=1, source_target_pairs={{0,4},{4,8},{8,12},{12,16},{16,20},{20,24},{24,28},{28,0},{1,5},{5... | collective-permute-start | bytes 88712 | tf_op jit(solution)/shard_map/ppermute | solution.py:32
  564.2 36.1 %collective-permute-start.31 = (f32[1,800,96]{1,2,0:T(8,128)S(1)}, f32[1,800,96]{1,2,0:T(8,128)S(1)}, u32[]{:S(2)}, u32[]{:S(2)}) collective-permute-start(f32[1,800,96]{1,2,0:T(8,128)S(1)} %get-tuple-element.759), channel_id=1, source_target_pairs={{0,1},{1,2},{2,3},{4,5},{5,6},{6,7},{8,9},{9,10},{10,11},{12,13},{... | collective-permute-start | bytes 921608 | tf_op jit(solution)/shard_map/ppermute | solution.py:21
  566.5 33.8 %collective-permute-start.30 = (f32[1,800,96]{1,2,0:T(8,128)S(1)}, f32[1,800,96]{1,2,0:T(8,128)S(1)}, u32[]{:S(2)}, u32[]{:S(2)}) collective-permute-start(f32[1,800,96]{1,2,0:T(8,128)S(1)} %get-tuple-element.759), channel_id=1, source_target_pairs={{1,0},{2,1},{3,2},{5,4},{6,5},{7,6},{9,8},{10,9},{11,10},{13,12},{... | collective-permute-start | bytes 921608 | tf_op jit(solution)/shard_map/ppermute | solution.py:23
  611.2 31.8 %collective-permute-start.32 = (f32[1,77,96]{2,1,0:T(8,128)S(1)}, f32[1,77,96]{2,1,0:T(8,128)S(1)}, u32[]{:S(2)}, u32[]{:S(2)}) collective-permute-start(f32[1,77,96]{2,1,0:T(8,128)S(1)} %get-tuple-element.924), channel_id=1, source_target_pairs={{0,28},{4,0},{8,4},{12,8},{16,12},{20,16},{24,20},{28,24},{1,29},{... | collective-permute-start | bytes 88712 | tf_op jit(solution)/shard_map/ppermute | solution.py:32
  640.8 84.9 %collective-permute-start.35 = (f32[1,77,96]{2,1,0:T(8,128)}, f32[1,77,96]{2,1,0:T(8,128)}, u32[]{:S(2)}, u32[]{:S(2)}) collective-permute-start(f32[1,77,96]{2,1,0:T(8,128)} %get-tuple-element.925), channel_id=1, source_target_pairs={{0,28},{4,0},{8,4},{12,8},{16,12},{20,16},{24,20},{28,24},{1,29},{... | collective-permute-start | bytes 88712 | tf_op jit(solution)/shard_map/ppermute | solution.py:32
  680.2 35.3 %collective-permute-start.34 = (f32[1,800,96]{1,2,0:T(8,128)S(1)}, f32[1,800,96]{1,2,0:T(8,128)S(1)}, u32[]{:S(2)}, u32[]{:S(2)}) collective-permute-start(f32[1,800,96]{1,2,0:T(8,128)S(1)} %get-tuple-element.760), channel_id=1, source_target_pairs={{0,1},{1,2},{2,3},{4,5},{5,6},{6,7},{8,9},{9,10},{10,11},{12,13},{... | collective-permute-start | bytes 921608 | tf_op jit(solution)/shard_map/ppermute | solution.py:21
  681.6 33.9 %collective-permute-start.33 = (f32[1,800,96]{1,2,0:T(8,128)S(1)}, f32[1,800,96]{1,2,0:T(8,128)S(1)}, u32[]{:S(2)}, u32[]{:S(2)}) collective-permute-start(f32[1,800,96]{1,2,0:T(8,128)S(1)} %get-tuple-element.760), channel_id=1, source_target_pairs={{1,0},{2,1},{3,2},{5,4},{6,5},{7,6},{9,8},{10,9},{11,10},{13,12},{... | collective-permute-start | bytes 921608 | tf_op jit(solution)/shard_map/ppermute | solution.py:23
  763.9 34.3 %collective-permute-start.38 = (f32[1,800,96]{1,2,0:T(8,128)S(1)}, f32[1,800,96]{1,2,0:T(8,128)S(1)}, u32[]{:S(2)}, u32[]{:S(2)}) collective-permute-start(f32[1,800,96]{1,2,0:T(8,128)S(1)} %get-tuple-element.758), channel_id=1, source_target_pairs={{0,1},{1,2},{2,3},{4,5},{5,6},{6,7},{8,9},{9,10},{10,11},{12,13},{... | collective-permute-start | bytes 921608 | tf_op jit(solution)/shard_map/ppermute | solution.py:21
  765.4 32.9 %collective-permute-start.37 = (f32[1,800,96]{1,2,0:T(8,128)S(1)}, f32[1,800,96]{1,2,0:T(8,128)S(1)}, u32[]{:S(2)}, u32[]{:S(2)}) collective-permute-start(f32[1,800,96]{1,2,0:T(8,128)S(1)} %get-tuple-element.758), channel_id=1, source_target_pairs={{1,0},{2,1},{3,2},{5,4},{6,5},{7,6},{9,8},{10,9},{11,10},{13,12},{... | collective-permute-start | bytes 921608 | tf_op jit(solution)/shard_map/ppermute | solution.py:23
  850.7 18.3 %collective-permute-start.43 = (f32[1,77,96]{2,1,0:T(8,128)S(1)}, f32[1,77,96]{2,1,0:T(8,128)S(1)}, u32[]{:S(2)}, u32[]{:S(2)}) collective-permute-start(f32[1,77,96]{2,1,0:T(8,128)S(1)} %copy-done.343), channel_id=1, source_target_pairs={{0,28},{4,0},{8,4},{12,8},{16,12},{20,16},{24,20},{28,24},{1,29},{... | collective-permute-start | bytes 88712 | tf_op jit(solution)/shard_map/ppermute | solution.py:32
  869.7 25.6 %collective-permute-start.44 = (f32[1,77,96]{2,1,0:T(8,128)S(1)}, f32[1,77,96]{2,1,0:T(8,128)S(1)}, u32[]{:S(2)}, u32[]{:S(2)}) collective-permute-start(f32[1,77,96]{2,1,0:T(8,128)S(1)} %get-tuple-element.919), channel_id=1, source_target_pairs={{0,28},{4,0},{8,4},{12,8},{16,12},{20,16},{24,20},{28,24},{1,29},{... | collective-permute-start | bytes 88712 | tf_op jit(solution)/shard_map/ppermute | solution.py:32
  927.9 17.9 collective-permute-start.46
  931.3 14.5 collective-permute-start.45
  1004.7 15.8 collective-permute-start.50
  1031.0 16.1 collective-permute-start.52
  1082.9 16.5 collective-permute-start.54
  1084.2 15.2 collective-permute-start.53
  1110.0 17.0 collective-permute-start.56
  1166.7 423.7 %all-reduce.417.cloned.1.call-start = ((), (), s32[]{:S(2)}) async-start(), calls=%async_computation.9 | async-start | bytes 2121728 | tf_op jit(solution)/shard_map/psum | solution.py:254
  1413.6 114.4 %collective-permute-start.58 = (f32[1,800,96]{1,2,0:T(8,128)S(1)}, f32[1,800,96]{1,2,0:T(8,128)S(1)}, u32[]{:S(2)}, u32[]{:S(2)}) collective-permute-start(f32[1,800,96]{1,2,0:T(8,128)S(1)} %get-tuple-element.765), channel_id=1, source_target_pairs={{0,1},{1,2},{2,3},{4,5},{5,6},{6,7},{8,9},{9,10},{10,11},{12,13},{... | collective-permute-start | bytes 921608 | tf_op jit(solution)/shard_map/ppermute | solution.py:21
  1415.0 112.9 %collective-permute-start.57 = (f32[1,800,96]{1,2,0:T(8,128)S(1)}, f32[1,800,96]{1,2,0:T(8,128)S(1)}, u32[]{:S(2)}, u32[]{:S(2)}) collective-permute-start(f32[1,800,96]{1,2,0:T(8,128)S(1)} %get-tuple-element.765), channel_id=1, source_target_pairs={{1,0},{2,1},{3,2},{5,4},{6,5},{7,6},{9,8},{10,9},{11,10},{13,12},{... | collective-permute-start | bytes 921608 | tf_op jit(solution)/shard_map/ppermute | solution.py:23
  1538.0 118.0 %reduce-scatter.11.cloned.1.call-start = ((), (), s32[]{:S(2)}) async-start(), calls=%async_computation.5 | async-start | bytes 12902400 | tf_op jit(solution)/shard_map/reduce_scatter | solution.py:272
  1570.5 142.2 %reduce-scatter.13.cloned.1.call-start = ((), (), s32[]{:S(2)}) async-start(), calls=%async_computation.6 | async-start | bytes 2048000
  1573.7 182.5 %all-reduce.415.cloned.1.call-start = ((), (), s32[]{:S(2)}) async-start(), calls=%async_computation.8 | async-start | bytes 2121728 | tf_op jit(solution)/shard_map/psum | solution.py:253
  1590.5 204.4 %reduce-scatter.15.cloned.1.call-start = ((), (), s32[]{:S(2)}) async-start(), calls=%async_computation.7 | async-start | bytes 2048000
  (609 other events, 7327.0 us)
Sparse Core Ops, SparseCore 0:
  1166.8 85.3 reduce-scatter.8
  1570.6 85.3 reduce-scatter.10
  1658.3 37.8 reduce-scatter.12
  1700.0 56.1 all-reduce.414
  1759.0 35.8 reduce-scatter.14
Sparse Core Ops, SparseCore 1:
  1538.1 52.3 all-reduce.416
